TPU v7x, 512 devices: a whole 4x8x8 slice. The times are simulated.
512 devices in a mesh: gx: 16 (over y, core), gy: 8 (over z), gz: 4 (over x).
Axes of the slice: x: 4, y: 8, z: 8, core: 2. Of those that a mesh axis runs over, the one named last changes fastest.
Arguments:
- noise: float32 [32, 64, 64, 512], P(None, 'gx', 'gy', 'gz'), may hold values from -32 to 32
- basis: float32 [192, 64, 64, 512], P(None, 'gx', 'gy', 'gz'), may hold values from -5 to 5
- conductivity: float32 [64, 64, 512], P('gx', 'gy', 'gz'), may hold values from 0.2 to 2
- reaction: float32 [64, 64, 512], P('gx', 'gy', 'gz'), may hold values from 0.05 to 0.5
Outputs:
- new_block: float32 [32, 64, 64, 512], P(None, 'gx', 'gy', 'gz')
- factor: float32 [32, 32], replicated
- projection: float32 [192, 32], replicated
All inputs are finite; a program needn't handle non-finite values.
Results may differ from a plain program's by a relative error of at most 0.00012.
Values sent between devices are 32-bit elements; how exact they have to be, the bound alone decides.
No kernel may reach another device: no remote copies, remote signals or barrier semaphores. Data moves between devices by JAX's collectives and lax.ppermute only.
A program may use at most 64 MiB of HBM per device.

v0:
```python
import jax
import jax.numpy as jnp
from jax import lax
from jax.sharding import PartitionSpec as P


def padded(value, sides, width):
    for axis, dim in sides:
        size, length = (lax.axis_size(axis), value.shape[dim])
        up = [(i, (i + 1) % size) for i in range(size - 1)]
        down = [(j, i) for i, j in up]
        last = lax.slice_in_dim(value, length - width, length, axis=dim)
        initial = lax.slice_in_dim(value, 0, width, axis=dim)
        before = lax.ppermute(last, axis, up)
        after = lax.ppermute(initial, axis, down)
        value = jnp.concatenate([before, value, after], axis=dim)
    return value


def stencil(field_pad, theta_pad, reaction_core):
    theta_core = theta_pad[1:-1, 1:-1, 1:-1]
    value_core = field_pad[:, 1:-1, 1:-1, 1:-1]
    result = reaction_core * value_core
    diagonal = reaction_core
    offsets = (
        (slice(2, None), slice(1, -1), slice(1, -1)),
        (slice(None, -2), slice(1, -1), slice(1, -1)),
        (slice(1, -1), slice(2, None), slice(1, -1)),
        (slice(1, -1), slice(None, -2), slice(1, -1)),
        (slice(1, -1), slice(1, -1), slice(2, None)),
        (slice(1, -1), slice(1, -1), slice(None, -2)),
    )
    for slicer in offsets:
        face_value = 0.5 * (theta_core + theta_pad[slicer])
        result = result + face_value * (value_core - field_pad[(slice(None),) + slicer])
        diagonal = diagonal + face_value
    return (result, diagonal)


def rim_layer(field):
    return padded(field, (("gx", 1), ("gy", 2), ("gz", 3)), 1)


def shards(noise, basis, conductivity, reaction):
    highest = lax.Precision.HIGHEST
    columns = noise.shape[0]
    span_x, span_y, span_z = (noise.shape[1], noise.shape[2], noise.shape[3])
    cell_total = float(
        span_x * span_y * span_z * lax.axis_size("gx") * lax.axis_size("gy") * lax.axis_size("gz")
    )
    extended = rim_layer(jnp.concatenate([noise, conductivity[None]], axis=0))
    theta_pad = extended[columns]
    first, diagonal = stencil(extended[:columns], theta_pad, reaction)
    image, unused = stencil(rim_layer(first / diagonal), theta_pad, reaction)
    basis_flat = basis.reshape(basis.shape[0], -1)
    image_flat = image.reshape(columns, -1)

    def local_product(left, right):
        return lax.dot_general(left, right, (((1,), (1,)), ((), ())), precision=highest)

    def remove(block, coeff):
        return block - lax.dot_general(
            coeff, basis_flat, (((0,), (0,)), ((), ())), precision=highest
        )

    def project(block):
        return lax.psum(local_product(basis_flat, block), ("gx", "gy", "gz")) / cell_total

    def gram_sum(block):
        return lax.psum(local_product(block, block), ("gx", "gy", "gz")) / cell_total

    coeff_one = project(image_flat)
    image_one = remove(image_flat, coeff_one)
    coeff_two = project(image_one)
    image_two = remove(image_one, coeff_two)
    gram_two = gram_sum(image_two)
    lower_one = jnp.linalg.cholesky(gram_two)
    middle = jax.scipy.linalg.solve_triangular(lower_one, image_two, lower=True)
    lower_two = jnp.linalg.cholesky(gram_sum(middle))
    new_block = jax.scipy.linalg.solve_triangular(lower_two, middle, lower=True)
    factor = jnp.dot(lower_two.T, lower_one.T, precision=highest)
    return (new_block.reshape(noise.shape), factor, coeff_one + coeff_two)


def solution(mesh):
    return jax.shard_map(
        shards,
        mesh=mesh,
        in_specs=(
            P(None, "gx", "gy", "gz"),
            P(None, "gx", "gy", "gz"),
            P("gx", "gy", "gz"),
            P("gx", "gy", "gz"),
        ),
        out_specs=(P(None, "gx", "gy", "gz"), P(), P()),
        check_vma=False,
    )
```

profile of v0, /device:TPU:1, one launch (start us, length us, event | category | flops | bytes accessed | tf_op | source)
XLA Modules:
  0.0 507.3 jit_solution(3330146122280983451)
XLA Ops:
  0.6 1.2 copy_dynamic-update-slice_fusion
  1.8 0.7 copy_dynamic-update-slice_fusion.1
  2.5 0.2 fusion.94
  2.8 4.6 collective-permute-start
  7.4 5.5 %collective-permute-start.1 = (f32[33,1,8,128]{3,1,2,0:T(1,128)S(1)}, f32[33,1,8,128]{3,1,2,0:T(1,128)S(1)}, u32[]{:S(2)}, u32[]{:S(2)}) collective-permute-start(f32[33,1,8,128]{3,1,2,0:T(1,128)S(1)} %get-tuple-element.21), channel_id=1, source_target_pairs={{32,0},{64,32},{96,64},{128,96},{160,128},{192,160},{224,192},{256... | collective-permute-start | bytes 405512 | tf_op jit(solution)/shard_map/ppermute | solution.py:15
  12.8 1.0 collective-permute-done.1
  13.9 3.9 collective-permute-start.2
  17.8 1.3 collective-permute-start.3
  19.1 0.7 collective-permute-done.2
  19.8 4.4 collective-permute-done.3
  24.2 0.7 copy-done.7
  24.8 0.4 pad_maximum_fusion
  25.2 0.4 fusion.92
  25.7 0.6 copy.33
  26.3 1.3 collective-permute-start.5
  27.5 0.6 copy.32
  28.1 4.6 collective-permute-start.4
  32.7 0.8 copy.35
  33.5 1.5 copy.34
  35.0 0.9 fusion.53
  36.2 5.2 %fusion.36 = f32[32,4,8,128]{3,1,2,0:T(4,128)S(1)} fusion(f32[33,6,10,1]{3,1,2,0:T(8,128)S(1)} %copy.34, f32[33,6,1,128]{3,1,2,0:T(8,128)S(1)} %copy-done.8, f32[33,6,1,128]{3,1,2,0:T(8,128)S(1)} %copy-done.6, f32[33,1,8,128]{3,1,2,0:T(1,128)S(1)} %collective-permute-done.1, f32[33,4,8,128]{3,1,2,0:T(4,128)S(1)} %copy_dynamic-update-slice_fusion.1, ...), kind=kLoop, calls=%fused_computation.56 | loop fusion | flops 4980736 | bytes 2209248 | tf_op jit(solution)/shard_map/div | solution.py:54
  41.4 0.2 fusion.95
  41.6 4.3 collective-permute-start.7
  45.9 1.9 collective-permute-start.6
  47.8 4.3 collective-permute-done.6
  52.3 4.0 collective-permute-start.9
  56.3 1.3 collective-permute-start.8
  57.6 0.6 collective-permute-done.9
  58.2 5.6 %collective-permute-done.8 = f32[32,6,1,128]{3,1,2,0:T(8,128)S(1)} collective-permute-done((f32[32,6,1,128]{3,1,2,0:T(8,128)S(1)}, f32[32,6,1,128]{3,1,2,0:T(8,128)S(1)}, u32[]{:S(2)}, u32[]{:S(2)}) %collective-permute-start.8) | collective-permute-done | bytes 98336 | tf_op jit(solution)/shard_map/ppermute | solution.py:15
  63.9 0.6 copy-done.9
  64.5 0.4 pad_maximum_fusion.1
  64.9 0.4 fusion.93
  65.3 0.5 copy.45
  65.8 1.3 collective-permute-start.10
  67.1 0.5 copy.47
  67.6 4.8 collective-permute-start.11
  72.5 1.6 copy.46
  74.1 1.6 copy.48
  75.8 5.8 %fusion.17 = f32[32,4,8,128]{3,1,2,0:T(4,128)S(1)} fusion(f32[32,4,8,128]{3,1,2,0:T(4,128)} %copy-done.1, f32[32,6,10,1]{3,1,2,0:T(8,128)} %copy.48, f32[32,6,1,128]{3,1,2,0:T(8,128)} %copy-done.9, f32[32,6,1,128]{3,1,2,0:T(8,128)S(1)} %collective-permute-done.9, f32[32,1,8,128]{3,1,2,0:T(1,128)S(1)} %collective-permute-done.6, ...), kind=kLoop, calls=%fused_computation.19 | loop fusion | flops 4849664 | bytes 1637376 | tf_op jit(solution)/shard_map/add | solution.py:35
  81.6 0.8 copy.49
  82.4 4.3 fusion.9
  86.8 101.9 %psum.28 = f32[192,32]{0,1:T(8,128)S(1)} all-reduce(f32[192,32]{0,1:T(8,128)S(1)} %fusion.9), channel_id=1, replica_groups=mesh['gx'=16,'gy'=8,'gz'=4] {'gx','gy','gz'}, use_global_device_ids=true, to_apply=%region_0.0 | all-reduce | flops 6144 | bytes 49152 | tf_op jit(solution)/shard_map/psum | solution.py:67
  188.7 4.8 convolution_subtract_fusion.1
  193.5 0.8 copy-done.3
  194.3 4.0 fusion.12
  198.4 94.7 %psum.29 = f32[192,32]{0,1:T(8,128)S(1)} all-reduce(f32[192,32]{0,1:T(8,128)S(1)} %fusion.12), channel_id=1, replica_groups=mesh['gx'=16,'gy'=8,'gz'=4] {'gx','gy','gz'}, use_global_device_ids=true, to_apply=%region_1.0 | all-reduce | flops 6144 | bytes 49152 | tf_op jit(solution)/shard_map/psum | solution.py:67
  293.1 4.7 convolution_subtract_fusion
  297.8 0.7 multiply_add_fusion
  298.6 0.6 fusion.96
  299.2 95.3 %psum.30 = f32[32,32]{0,1:T(8,128)S(1)} all-reduce(f32[32,32]{0,1:T(8,128)S(1)} %fusion.96), channel_id=1, replica_groups=mesh['gx'=16,'gy'=8,'gz'=4] {'gx','gy','gz'}, use_global_device_ids=true, to_apply=%region_2.0 | all-reduce | flops 1024 | bytes 8192 | tf_op jit(solution)/shard_map/psum | solution.py:70
  394.5 2.9 cholesky.44
  397.5 0.7 compare_reduce_fusion.1
  398.1 0.6 fusion.70
  398.8 2.4 custom-call.6
  401.2 1.7 fusion.64
  402.9 0.6 fusion.97
  403.5 93.4 %psum.31 = f32[32,32]{0,1:T(8,128)S(1)} all-reduce(f32[32,32]{0,1:T(8,128)S(1)} %fusion.97), channel_id=1, replica_groups=mesh['gx'=16,'gy'=8,'gz'=4] {'gx','gy','gz'}, use_global_device_ids=true, to_apply=%region_5.8 | all-reduce | flops 1024 | bytes 8192 | tf_op jit(solution)/shard_map/psum | solution.py:70
  497.0 2.9 cholesky.55
  499.9 0.6 compare_reduce_fusion
  500.6 2.1 fusion.75
  502.7 0.7 select_bitcast_fusion
  503.3 2.4 custom-call.7
  505.8 0.7 convolution_bitcast_fusion
  506.4 0.9 copy.61
  (48 shorter events, 0.8 us)
Async XLA Ops:
  2.8 10.1 %collective-permute-start = (f32[33,1,8,128]{3,1,2,0:T(1,128)S(1)}, f32[33,1,8,128]{3,1,2,0:T(1,128)S(1)}, u32[]{:S(2)}, u32[]{:S(2)}) collective-permute-start(f32[33,1,8,128]{3,1,2,0:T(1,128)S(1)} %get-tuple-element.20), channel_id=1, source_target_pairs={{0,32},{32,64},{64,96},{96,128},{128,160},{160,192},{192,224},{224... | collective-permute-start | bytes 405512 | tf_op jit(solution)/shard_map/ppermute | solution.py:14
  7.4 6.4 %collective-permute-start.1 = (f32[33,1,8,128]{3,1,2,0:T(1,128)S(1)}, f32[33,1,8,128]{3,1,2,0:T(1,128)S(1)}, u32[]{:S(2)}, u32[]{:S(2)}) collective-permute-start(f32[33,1,8,128]{3,1,2,0:T(1,128)S(1)} %get-tuple-element.21), channel_id=1, source_target_pairs={{32,0},{64,32},{96,64},{128,96},{160,128},{192,160},{224,192},{256... | collective-permute-start | bytes 405512 | tf_op jit(solution)/shard_map/ppermute | solution.py:15
  13.9 5.9 %collective-permute-start.2 = (f32[33,6,1,128]{3,1,2,0:T(8,128)S(1)}, f32[33,6,1,128]{3,1,2,0:T(8,128)S(1)}, u32[]{:S(2)}, u32[]{:S(2)}) collective-permute-start(f32[33,6,1,128]{3,1,2,0:T(8,128)S(1)} %get-tuple-element.16), channel_id=1, source_target_pairs={{0,4},{4,8},{8,12},{12,16},{16,20},{20,24},{24,28},{1,5},{5,9},{9,... | collective-permute-start | bytes 304136 | tf_op jit(solution)/shard_map/ppermute | solution.py:14
  17.8 6.4 %collective-permute-start.3 = (f32[33,6,1,128]{3,1,2,0:T(8,128)S(1)}, f32[33,6,1,128]{3,1,2,0:T(8,128)S(1)}, u32[]{:S(2)}, u32[]{:S(2)}) collective-permute-start(f32[33,6,1,128]{3,1,2,0:T(8,128)S(1)} %get-tuple-element.17), channel_id=1, source_target_pairs={{4,0},{8,4},{12,8},{16,12},{20,16},{24,20},{28,24},{5,1},{9,5},{13... | collective-permute-start | bytes 304136 | tf_op jit(solution)/shard_map/ppermute | solution.py:15
  19.8 4.4 copy-start.5
  24.2 0.7 copy-start.7
  26.3 6.5 %collective-permute-start.5 = (f32[33,6,10,1]{0,3,2,1:T(1,128)S(1)}, f32[33,6,10,1]{0,3,2,1:T(1,128)S(1)}, u32[]{:S(2)}, u32[]{:S(2)}) collective-permute-start(f32[33,6,10,1]{0,3,2,1:T(1,128)S(1)} %copy.33), channel_id=1, source_target_pairs={{1,0},{2,1},{3,2},{5,4},{6,5},{7,6},{9,8},{10,9},{11,10},{13,12},{... | collective-permute-start | bytes 23768 | tf_op jit(solution)/shard_map/ppermute | solution.py:15
  28.1 5.4 %collective-permute-start.4 = (f32[33,6,10,1]{0,3,2,1:T(1,128)S(1)}, f32[33,6,10,1]{0,3,2,1:T(1,128)}, u32[]{:S(2)}, u32[]{:S(2)}) collective-permute-start(f32[33,6,10,1]{0,3,2,1:T(1,128)S(1)} %copy.32), channel_id=1, source_target_pairs={{0,1},{1,2},{2,3},{4,5},{5,6},{6,7},{8,9},{9,10},{10,11},{12,13},{... | collective-permute-start | bytes 23768 | tf_op jit(solution)/shard_map/ppermute | solution.py:14
  35.0 1.0 copy-start.16
  35.0 1.1 copy-start.4
  35.0 1.1 copy-start.6
  35.0 1.1 copy-start.8
  36.1 5.3 %copy-start.10 = (f32[4,8,128]{2,0,1:T(4,128)}, f32[4,8,128]{2,0,1:T(4,128)S(1)}, u32[]{:S(2)}) copy-start(f32[4,8,128]{2,0,1:T(4,128)S(1)} %get-tuple-element.7) | copy-start | bytes 49156
  36.1 5.3 %copy-start.11 = (f32[4,8,128]{2,0,1:T(4,128)}, f32[4,8,128]{2,0,1:T(4,128)S(1)}, u32[]{:S(2)}) copy-start(f32[4,8,128]{2,0,1:T(4,128)S(1)} %get-tuple-element.8) | copy-start | bytes 49156
  36.1 5.3 %copy-start.12 = (f32[4,8,128]{2,0,1:T(4,128)}, f32[4,8,128]{2,0,1:T(4,128)S(1)}, u32[]{:S(2)}) copy-start(f32[4,8,128]{2,0,1:T(4,128)S(1)} %get-tuple-element.9) | copy-start | bytes 49156
  36.1 5.3 %copy-start.13 = (f32[4,8,128]{2,0,1:T(4,128)}, f32[4,8,128]{2,0,1:T(4,128)S(1)}, u32[]{:S(2)}) copy-start(f32[4,8,128]{2,0,1:T(4,128)S(1)} %get-tuple-element.10) | copy-start | bytes 49156
  36.1 5.3 %copy-start.14 = (f32[4,8,128]{2,0,1:T(4,128)}, f32[4,8,128]{2,0,1:T(4,128)S(1)}, u32[]{:S(2)}) copy-start(f32[4,8,128]{2,0,1:T(4,128)S(1)} %get-tuple-element.11) | copy-start | bytes 49156
  36.1 5.3 %copy-start.15 = (f32[4,8,128]{2,0,1:T(4,128)}, f32[4,8,128]{2,0,1:T(4,128)S(1)}, u32[]{:S(2)}) copy-start(f32[4,8,128]{2,0,1:T(4,128)S(1)} %get-tuple-element.24) | copy-start | bytes 49156
  41.4 22.4 %copy-start.1 = (f32[32,4,8,128]{3,1,2,0:T(4,128)}, f32[32,4,8,128]{3,1,2,0:T(4,128)S(1)}, u32[]{:S(2)}) copy-start(f32[32,4,8,128]{3,1,2,0:T(4,128)S(1)} %fusion.36) | copy-start | bytes 1572868
  41.6 6.2 %collective-permute-start.7 = (f32[32,1,8,128]{3,1,2,0:T(1,128)S(1)}, f32[32,1,8,128]{3,1,2,0:T(1,128)S(1)}, u32[]{:S(2)}, u32[]{:S(2)}) collective-permute-start(f32[32,1,8,128]{3,1,2,0:T(1,128)S(1)} %get-tuple-element.22), channel_id=1, source_target_pairs={{0,32},{32,64},{64,96},{96,128},{128,160},{160,192},{192,224},{224... | collective-permute-start | bytes 393224 | tf_op jit(solution)/shard_map/ppermute | solution.py:14
  45.9 6.3 %collective-permute-start.6 = (f32[32,1,8,128]{3,1,2,0:T(1,128)S(1)}, f32[32,1,8,128]{3,1,2,0:T(1,128)S(1)}, u32[]{:S(2)}, u32[]{:S(2)}) collective-permute-start(f32[32,1,8,128]{3,1,2,0:T(1,128)S(1)} %get-tuple-element.23), channel_id=1, source_target_pairs={{32,0},{64,32},{96,64},{128,96},{160,128},{192,160},{224,192},{256... | collective-permute-start | bytes 393224 | tf_op jit(solution)/shard_map/ppermute | solution.py:15
  52.3 5.9 %collective-permute-start.9 = (f32[32,6,1,128]{3,1,2,0:T(8,128)S(1)}, f32[32,6,1,128]{3,1,2,0:T(8,128)S(1)}, u32[]{:S(2)}, u32[]{:S(2)}) collective-permute-start(f32[32,6,1,128]{3,1,2,0:T(8,128)S(1)} %get-tuple-element.18), channel_id=1, source_target_pairs={{0,4},{4,8},{8,12},{12,16},{16,20},{20,24},{24,28},{1,5},{5,9},{9,... | collective-permute-start | bytes 294920 | tf_op jit(solution)/shard_map/ppermute | solution.py:14
  56.3 7.6 %collective-permute-start.8 = (f32[32,6,1,128]{3,1,2,0:T(8,128)S(1)}, f32[32,6,1,128]{3,1,2,0:T(8,128)S(1)}, u32[]{:S(2)}, u32[]{:S(2)}) collective-permute-start(f32[32,6,1,128]{3,1,2,0:T(8,128)S(1)} %get-tuple-element.19), channel_id=1, source_target_pairs={{4,0},{8,4},{12,8},{16,12},{20,16},{24,20},{28,24},{5,1},{9,5},{13... | collective-permute-start | bytes 294920 | tf_op jit(solution)/shard_map/ppermute | solution.py:15
  63.9 0.6 copy-start.9
  65.8 6.7 %collective-permute-start.10 = (f32[32,6,10,1]{0,3,2,1:T(1,128)S(1)}, f32[32,6,10,1]{0,3,2,1:T(1,128)S(1)}, u32[]{:S(2)}, u32[]{:S(2)}) collective-permute-start(f32[32,6,10,1]{0,3,2,1:T(1,128)S(1)} %copy.45), channel_id=1, source_target_pairs={{1,0},{2,1},{3,2},{5,4},{6,5},{7,6},{9,8},{10,9},{11,10},{13,12},{... | collective-permute-start | bytes 23048 | tf_op jit(solution)/shard_map/ppermute | solution.py:15
  67.6 6.5 %collective-permute-start.11 = (f32[32,6,10,1]{0,3,2,1:T(1,128)S(1)}, f32[32,6,10,1]{0,3,2,1:T(1,128)S(1)}, u32[]{:S(2)}, u32[]{:S(2)}) collective-permute-start(f32[32,6,10,1]{0,3,2,1:T(1,128)S(1)} %copy.47), channel_id=1, source_target_pairs={{0,1},{1,2},{2,3},{4,5},{5,6},{6,7},{8,9},{9,10},{10,11},{12,13},{... | collective-permute-start | bytes 23048 | tf_op jit(solution)/shard_map/ppermute | solution.py:14
  75.8 6.7 %copy-start = (f32[192,4,8,128]{3,2,1,0:T(8,128)S(1)}, f32[192,4,8,128]{3,2,1,0:T(8,128)}, u32[]{:S(2)}) copy-start(f32[192,4,8,128]{3,2,1,0:T(8,128)} %param.8) | copy-start | bytes 9437188
  193.5 0.8 copy-start.3
  297.8 0.8 copy-start.2
where the time goes:
time: 509 us; the launch traced here: 507 us
  blocking collectives  385 us (76%)
  starting transfers between devices  38.7 us (8%)
  other arithmetic  27 us (5%)
  matrix products  23.5 us (5%)
  waiting for transfers between devices  16.7 us (3%)
  local copies, waits for them, and re-layouts  15 us (3%)
    psum x2, blocking collectives, project(): lax.psum(local_product(basis_flat, block), ('gx', 'gy', 'gz')) / cell_total  197 us
    psum x2, blocking collectives, gram_sum(): lax.psum(local_product(block, block), ('gx', 'gy', 'gz')) / cell_total  189 us
    ppermute x6, starting transfers between devices, padded(): before = lax.ppermute(last, axis, up)  26.2 us
    ppermute x6, waiting for transfers between devices, padded(): after = lax.ppermute(initial, axis, down)  15.4 us
    ppermute x6, starting transfers between devices, padded(): after = lax.ppermute(initial, axis, down)  12.5 us
  transfers between devices with their start and end apart: 12, of which 6 were waited for; matrix products, arithmetic and copies ran while one was open for 1% of the time, Pallas kernels for 0%

commit v1 on v0

v1 whole, which is shorter than its diff:
```python
import jax
import jax.numpy as jnp
from jax import lax
from jax.experimental import pallas as pl
from jax.experimental.pallas import tpu as pltpu
from jax.sharding import Mesh, PartitionSpec as P

GX = ("y", "core")
CHIP_X = ("core", "gz")
HIGHEST = lax.Precision.HIGHEST
F32 = jnp.float32


def shifted(value, axis, forward):
    size = lax.axis_size(axis)
    up = [(i, (i + 1) % size) for i in range(size - 1)]
    pairs = up if forward else [(j, i) for i, j in up]
    return lax.ppermute(value, axis, pairs)


def exchange(faces):
    xlo, xhi, ylo, yhi, zlo, zhi = faces
    return (
        shifted(xhi, GX, True),
        shifted(xlo, GX, False),
        shifted(yhi, "gy", True),
        shifted(ylo, "gy", False),
        shifted(zhi, "gz", True),
        shifted(zlo, "gz", False),
    )


def pack_faces(ref, row, rows, outs, at):
    xlo, xhi, ylo, yhi, zlo, zhi = outs
    fields, span_x, span_y, span_z = ref.shape
    xlo[at : at + fields] = ref[:, 0]
    xhi[at : at + fields] = ref[:, span_x - 1]
    ylo[at : at + fields] = ref[:, :, 0, :]
    yhi[at : at + fields] = ref[:, :, span_y - 1, :]
    step = min(rows, fields * span_x * span_y)
    per = step // (span_x * span_y)
    for k in range(fields // per):
        turned = ref[k * per : (k + 1) * per].reshape(step, span_z).T
        zlo[row + k : row + k + 1, :step] = turned[:1]
        zhi[row + k : row + k + 1, :step] = turned[span_z - 1 :]


def z_columns(low, high, row, step):
    lanes = low.shape[1]
    below = jnp.broadcast_to(low[row : row + 1, :step], (lanes, step))
    above = jnp.broadcast_to(high[row : row + 1, :step], (lanes, step))
    first = lax.broadcasted_iota(jnp.int32, (lanes, step), 0) < lanes // 2
    return jnp.where(first, below, above).T


def neighbours(value, halo, lo, hi, row, step):
    before_x, after_x, before_y, after_y, before_z, after_z = halo
    shape = value.shape
    span_y, span_z = shape[2:]
    at_y = lax.broadcasted_iota(jnp.int32, shape, 2)
    at_z = lax.broadcasted_iota(jnp.int32, shape, 3)
    x_minus = jnp.concatenate([before_x[lo:hi][:, None], value[:, :-1]], axis=1)
    x_plus = jnp.concatenate([value[:, 1:], after_x[lo:hi][:, None]], axis=1)
    y_minus = jnp.where(at_y == 0, before_y[lo:hi][:, :, None, :], pltpu.roll(value, 1, 2))
    y_plus = jnp.where(at_y == span_y - 1, after_y[lo:hi][:, :, None, :], pltpu.roll(value, span_y - 1, 2))
    edge = z_columns(before_z, after_z, row, step).reshape(shape)
    z_minus = jnp.where(at_z == 0, edge, pltpu.roll(value, 1, 3))
    z_plus = jnp.where(at_z == span_z - 1, edge, pltpu.roll(value, span_z - 1, 3))
    return (x_plus, x_minus, y_plus, y_minus, z_plus, z_minus)


def face_values(theta, halo, fields, rows):
    others = neighbours(theta[...][None], halo, fields, fields + 1, rows, theta.shape[0] * theta.shape[1])
    return [0.5 * (theta[...] + other[0]) for other in others]


def apply_operator(value, reaction, values, halo, lo, row, step):
    others = neighbours(value, halo, lo, lo + value.shape[0], row, step)
    result = reaction * value
    for face, other in zip(values, others):
        result = result + face * (value - other)
    return result


def face_kernel(noise, theta, *outs):
    fields = noise.shape[0]
    blocks = fields * noise.shape[1] * noise.shape[2] // 128
    pack_faces(noise, 0, 128, outs, 0)
    for ref, face in zip(outs[:2], (theta[0], theta[theta.shape[0] - 1])):
        ref[fields] = face
    outs[2][fields] = theta[:, 0, :]
    outs[3][fields] = theta[:, theta.shape[1] - 1, :]
    step = theta.shape[0] * theta.shape[1]
    turned = theta[...].reshape(step, theta.shape[2]).T
    outs[4][blocks : blocks + 1, :step] = turned[:1]
    outs[5][blocks : blocks + 1, :step] = turned[theta.shape[2] - 1 :]


def first_kernel(noise, theta, reaction, *refs):
    halo, scaled, outs = refs[:6], refs[6], refs[7:]
    fields, span_x, span_y, span_z = noise.shape
    blocks = fields * span_x * span_y // 128
    per = fields // blocks
    values = face_values(theta, halo, fields, blocks)
    diagonal = reaction[...]
    for face in values:
        diagonal = diagonal + face
    inverse = 1.0 / diagonal
    for k in range(blocks):
        value = noise[k * per : (k + 1) * per]
        first = apply_operator(value, reaction[...], values, halo, k * per, k, 128)
        scaled[k * per : (k + 1) * per] = first * inverse
    pack_faces(scaled, 0, 128, outs, 0)


def second_kernel(scaled, theta, reaction, *refs):
    halo, theta_halo, image = refs[:6], refs[6:12], refs[12]
    fields, span_x, span_y, span_z = scaled.shape
    blocks = fields * span_x * span_y // 128
    per = fields // blocks
    values = face_values(theta, theta_halo, fields, blocks)
    for k in range(blocks):
        value = scaled[k * per : (k + 1) * per]
        image[k * per : (k + 1) * per] = apply_operator(value, reaction[...], values, halo, k * per, k, 128)


def call(kernel, outs, *args):
    return pl.pallas_call(
        kernel,
        out_shape=[jax.ShapeDtypeStruct(s, F32) for s in outs],
        in_specs=[pl.BlockSpec(memory_space=pltpu.VMEM)] * len(args),
        out_specs=[pl.BlockSpec(memory_space=pltpu.VMEM)] * len(outs),
        cost_estimate=pl.CostEstimate(flops=1 << 22, bytes_accessed=1 << 21, transcendentals=0),
    )(*args)


def face_shapes(shape, extra):
    fields, span_x, span_y, span_z = shape
    n = fields + extra
    blocks = fields * span_x * span_y // 128
    z_rows = blocks + 8 * extra
    return [(n, span_y, span_z)] * 2 + [(n, span_x, span_z)] * 2 + [(z_rows, span_z)] * 2


def spread_sum(value, axes):
    size = lax.axis_size(axes)
    copies = jnp.broadcast_to(value[None], (size,) + value.shape)
    return jnp.sum(lax.all_to_all(copies, axes, 0, 0), axis=0)


def total(rows):
    size = lax.axis_size(CHIP_X)
    pieces = rows.reshape(size, -1, rows.shape[1])
    piece = jnp.sum(lax.all_to_all(pieces, CHIP_X, 0, 0), axis=0)
    piece = spread_sum(spread_sum(piece, "gy"), "y")
    copies = jnp.broadcast_to(piece[None], (size,) + piece.shape)
    return lax.all_to_all(copies, CHIP_X, 0, 0).reshape(rows.shape)


def shards(noise, basis, conductivity, reaction):
    columns = noise.shape[0]
    shape = noise.shape
    stored = basis.shape[0]
    cell_total = float(
        shape[1] * shape[2] * shape[3] * lax.axis_size(GX) * lax.axis_size("gy") * lax.axis_size("gz")
    )
    halo = exchange(call(face_kernel, face_shapes(shape, 1), noise, conductivity))
    scaled, *faces = call(
        first_kernel, [shape] + face_shapes(shape, 0), noise, conductivity, reaction, *halo
    )
    next_halo = exchange(faces)
    (image,) = call(second_kernel, [shape], scaled, conductivity, reaction, *next_halo, *halo)
    basis_flat = basis.reshape(stored, -1)
    image_flat = image.reshape(columns, -1)

    def dot(left, right, dims):
        return lax.dot_general(left, right, ((dims[0], dims[1]), ((), ())), precision=HIGHEST)

    rows_by_rows = ((1,), (1,))
    plain = ((1,), (0,))
    gram = dot(basis_flat, basis_flat, rows_by_rows)
    cross = dot(image_flat, basis_flat, rows_by_rows)
    own = dot(image_flat, image_flat, rows_by_rows)
    width = 128
    rest = stored - width
    corner = jnp.concatenate(
        [cross[:, width:], jnp.pad(own, ((0, rest - columns), (0, rest - columns)))], axis=0
    )[:rest]
    packed = jnp.concatenate(
        [
            gram[:, :width],
            cross[:, :width],
            jnp.concatenate([gram[width:, width:], corner], axis=1),
            jnp.zeros((32, width), F32),
        ],
        axis=0,
    )
    packed = total(packed) / cell_total
    left = packed[:stored]
    tail = packed[stored + columns : stored + columns + rest]
    gram = jnp.concatenate(
        [left, jnp.concatenate([left[width:].T, tail[:, :rest]], axis=0)], axis=1
    )
    one = jnp.concatenate([packed[stored : stored + columns], tail[:columns, rest:]], axis=1)
    own = tail[columns : 2 * columns, rest : rest + columns]
    two = one - dot(one, gram, plain)
    left_over = two - dot(two, gram, plain)
    both = one + two
    square = own - dot(one, both, rows_by_rows) - dot(both, left_over, rows_by_rows)
    eye = jnp.eye(columns, dtype=F32)
    lower_one = jnp.linalg.cholesky(square)
    inverse_one = jax.scipy.linalg.solve_triangular(lower_one, eye, lower=True)
    middle = dot(dot(inverse_one, square, plain), inverse_one, rows_by_rows)
    lower_two = jnp.linalg.cholesky(middle)
    inverse = jax.scipy.linalg.solve_triangular(lower_two, inverse_one, lower=True)
    factor = dot(lower_one, lower_two, plain).T
    mixed = dot(inverse, both, plain)
    new_block = dot(inverse, image_flat, plain) - dot(mixed, basis_flat, plain)
    return (new_block.reshape(shape), factor, both.T)


def solution(mesh):
    grid = mesh.devices.reshape(mesh.devices.shape[0] // 2, 2, *mesh.devices.shape[1:])
    fine = Mesh(grid, ("y", "core", "gy", "gz"))
    return jax.shard_map(
        shards,
        mesh=fine,
        in_specs=(
            P(None, GX, "gy", "gz"),
            P(None, GX, "gy", "gz"),
            P(GX, "gy", "gz"),
            P(GX, "gy", "gz"),
        ),
        out_specs=(P(None, GX, "gy", "gz"), P(), P()),
        check_vma=False,
    )
```

time: 509 us -> 161 us (0.32)
  blocking collectives: 385 us -> 61.2 us
  waiting for transfers between devices: 16.7 us -> 4.57 us
  other arithmetic: 27 us -> 15.6 us
  local copies, waits for them, and re-layouts: 15 us -> 6.74 us
  Pallas kernels: 0 us -> 8.16 us
    psum x4 -> x0, blocking collectives: 385 us -> none  [the longest x2 197 us: project(): lax.psum(local_product(basis_flat, block), ('gx', 'gy', 'gz')) / cell_total]
    all_to_all x0 -> x4, blocking collectives: none -> 61.2 us  [the longest x2 39.4 us: spread_sum(): return jnp.sum(lax.all_to_all(copies, axes, 0, 0), axis=0)]
    ppermute x12, waiting for transfers between devices: 16.7 us -> 4.57 us  [shifted(): return lax.ppermute(value, axis, pairs)]
    pallas_call x0 -> x3, Pallas kernels: none -> 8.16 us  [call(): pl.pallas_call(kernel, out_shape=[jax.ShapeDtypeStruct(s, F32) for s in o...]
    add x3 -> x0, other arithmetic: 6.63 us -> none  [the longest x1 5.84 us: stencil(): result + face_value * (value_core - field_pad[(slice(None),) + slicer])]
    ppermute x4 -> x0, local copies, waits for them, and re-layouts: 5.53 us -> none  [the longest x2 3.14 us: padded(): before = lax.ppermute(last, axis, up)]
    dot_general x7 -> x13, matrix products: 21.1 us -> 26.5 us  [dot(): lax.dot_general(left, right, ((dims[0], dims[1]), ((), ())), precision=HI...]
    div x5 -> x3, other arithmetic: 5.18 us -> 0.03 us  [the longest x1 0.01 us: shards(): packed = total(packed) / cell_total]
  transfers between devices with their start and end apart: 12 -> 12, of which waited for: 6 -> 2; matrix products, arithmetic and copies ran while one was open for 1% -> 6% of each run, Pallas kernels for 0% -> 0%
where the time goes in v1:
time: 161 us; the launch traced here: 160 us
  blocking collectives  61.2 us (38%)
  starting transfers between devices  35.4 us (22%)
  matrix products  27 us (17%)
  other arithmetic  15.6 us (10%)
  Pallas kernels  8.16 us (5%)
  local copies, waits for them, and re-layouts  6.74 us (4%)
  waiting for transfers between devices  4.57 us (3%)
    all_to_all x2, blocking collectives, spread_sum(): return jnp.sum(lax.all_to_all(copies, axes, 0, 0), axis=0)  39.4 us
    ppermute x12, starting transfers between devices, shifted(): return lax.ppermute(value, axis, pairs)  35.4 us
    dot_general x13, matrix products, dot(): lax.dot_general(left, right, ((dims[0], dims[1]), ((), ())), precision=HI...  26.5 us
    all_to_all x1, blocking collectives, total(): return lax.all_to_all(copies, CHIP_X, 0, 0).reshape(rows.shape)  11 us
    all_to_all x1, blocking collectives, total(): piece = jnp.sum(lax.all_to_all(pieces, CHIP_X, 0, 0), axis=0)  10.8 us
    pallas_call x3, Pallas kernels, call(): pl.pallas_call(kernel, out_shape=[jax.ShapeDtypeStruct(s, F32) for s in o...  8.16 us
    unnamed x32, local copies, waits for them, and re-layouts  4.69 us
    ppermute x12, waiting for transfers between devices, shifted(): return lax.ppermute(value, axis, pairs)  4.57 us
  transfers between devices with their start and end apart: 12, of which 2 were waited for; matrix products, arithmetic and copies ran while one was open for 6% of the time, Pallas kernels for 0%

profile of v1, /device:TPU:1, one launch (start us, length us, event | category | flops | bytes accessed | tf_op | source)
XLA Modules:
  0.0 159.8 jit_solution(3969424943566784033)
XLA Ops:
  0.6 1.9 %shard_map.67 = (f32[33,8,128]{2,1,0:T(8,128)}, f32[33,8,128]{2,1,0:T(8,128)}, f32[33,4,128]{2,1,0:T(4,128)}, f32[33,4,128]{2,1,0:T(4,128)}, f32[16,128]{1,0:T(8,128)}, /*index=5*/f32[16,128]{1,0:T(8,128)}) custom-call(f32[32,4,8,128]{3,2,1,0:T(8,128)} %noise.3, f32[4,8,128]{2,1,0:T(8,128)} %theta.5), custom_call_target="tpu_custom_call" | custom-call | flops 4194304 | bytes 2097152 | tf_op jit(solution)/shard_map/pallas_call | solution.py:128
  2.6 4.6 %collective-permute-start = (f32[33,8,128]{2,1,0:T(8,128)}, f32[33,8,128]{2,1,0:T(8,128)S(1)}, u32[]{:S(2)}, u32[]{:S(2)}) collective-permute-start(f32[33,8,128]{2,1,0:T(8,128)} %get-tuple-element.18), channel_id=1, source_target_pairs={{0,32},{32,64},{64,96},{96,128},{128,160},{160,192},{192,224},{224... | collective-permute-start | bytes 405512 | tf_op jit(solution)/shard_map/ppermute | solution.py:18
  7.2 5.5 %collective-permute-start.1 = (f32[33,8,128]{2,1,0:T(8,128)}, f32[33,8,128]{2,1,0:T(8,128)S(1)}, u32[]{:S(2)}, u32[]{:S(2)}) collective-permute-start(f32[33,8,128]{2,1,0:T(8,128)} %get-tuple-element.19), channel_id=1, source_target_pairs={{32,0},{64,32},{96,64},{128,96},{160,128},{192,160},{224,192},{256... | collective-permute-start | bytes 405512 | tf_op jit(solution)/shard_map/ppermute | solution.py:18
  12.6 1.3 collective-permute-start.2
  13.9 1.3 collective-permute-start.3
  15.2 2.3 %collective-permute-start.4 = (f32[16,128]{1,0:T(8,128)}, f32[16,128]{1,0:T(8,128)S(1)}, u32[]{:S(2)}, u32[]{:S(2)}) collective-permute-start(f32[16,128]{1,0:T(8,128)} %get-tuple-element.22), channel_id=1, source_target_pairs={{0,1},{1,2},{2,3},{4,5},{5,6},{6,7},{8,9},{9,10},{10,11},{12,13},{... | collective-permute-start | bytes 24584 | tf_op jit(solution)/shard_map/ppermute | solution.py:18
  17.5 1.0 collective-permute-done.4.refs_4_.refs_10_
  18.5 0.6 copy-done.11
  19.1 1.5 collective-permute-start.5
  20.6 3.6 %collective-permute-done.5.refs_5_.refs_11_ = f32[16,128]{1,0:T(8,128)S(1)} collective-permute-done((f32[16,128]{1,0:T(8,128)}, f32[16,128]{1,0:T(8,128)S(1)}, u32[]{:S(2)}, u32[]{:S(2)}) %collective-permute-start.5) | collective-permute-done | bytes 8224 | tf_op jit(solution)/shard_map/ppermute | solution.py:18
  24.2 0.6 copy-done.12
  24.8 0.0 copy-done.5
  24.9 0.6 copy-done.3
  25.5 0.6 copy-done.4
  26.1 3.2 %shard_map.68 = (f32[32,4,8,128]{3,2,1,0:T(8,128)}, f32[32,8,128]{2,1,0:T(8,128)}, f32[32,8,128]{2,1,0:T(8,128)}, f32[32,4,128]{2,1,0:T(4,128)}, f32[32,4,128]{2...) custom-call(f32[32,4,8,128]{3,2,1,0:T(8,128)} %noise.3, f32[4,8,128]{2,1,0:T(8,128)} %theta.5, f32[4,8,128]{2,1,0:T(8,128)} %reaction.3, ...), custom_call_target="tpu_custom_call" | custom-call | flops 4194304 | bytes 2097152 | tf_op jit(solution)/shard_map/pallas_call | solution.py:128
  29.3 3.6 %collective-permute-start.10 = (f32[8,128]{1,0:T(8,128)}, f32[8,128]{1,0:T(8,128)S(1)}, u32[]{:S(2)}, u32[]{:S(2)}) collective-permute-start(f32[8,128]{1,0:T(8,128)} %get-tuple-element.29), channel_id=1, source_target_pairs={{0,1},{1,2},{2,3},{4,5},{5,6},{6,7},{8,9},{9,10},{10,11},{12,13},{... | collective-permute-start | bytes 12296 | tf_op jit(solution)/shard_map/ppermute | solution.py:18
  32.9 6.3 %collective-permute-start.6 = (f32[32,8,128]{2,1,0:T(8,128)}, f32[32,8,128]{2,1,0:T(8,128)S(1)}, u32[]{:S(2)}, u32[]{:S(2)}) collective-permute-start(f32[32,8,128]{2,1,0:T(8,128)} %get-tuple-element.25), channel_id=1, source_target_pairs={{0,32},{32,64},{64,96},{96,128},{128,160},{160,192},{192,224},{224... | collective-permute-start | bytes 393224 | tf_op jit(solution)/shard_map/ppermute | solution.py:18
  39.2 1.9 %collective-permute-start.7 = (f32[32,8,128]{2,1,0:T(8,128)}, f32[32,8,128]{2,1,0:T(8,128)S(1)}, u32[]{:S(2)}, u32[]{:S(2)}) collective-permute-start(f32[32,8,128]{2,1,0:T(8,128)} %get-tuple-element.26), channel_id=1, source_target_pairs={{32,0},{64,32},{96,64},{128,96},{160,128},{192,160},{224,192},{256... | collective-permute-start | bytes 393224 | tf_op jit(solution)/shard_map/ppermute | solution.py:18
  41.1 4.6 %collective-permute-start.8 = (f32[32,4,128]{2,1,0:T(4,128)}, f32[32,4,128]{2,1,0:T(4,128)S(1)}, u32[]{:S(2)}, u32[]{:S(2)}) collective-permute-start(f32[32,4,128]{2,1,0:T(4,128)} %get-tuple-element.27), channel_id=1, source_target_pairs={{0,4},{4,8},{8,12},{12,16},{16,20},{20,24},{24,28},{1,5},{5,9},{9,... | collective-permute-start | bytes 196616 | tf_op jit(solution)/shard_map/ppermute | solution.py:18
  45.8 1.3 collective-permute-start.9
  47.1 1.3 collective-permute-start.11
  48.4 8.8 %fusion.8 = f32[192,192]{1,0:T(8,128)S(1)} fusion(f32[192,4,8,128]{3,2,1,0:T(8,128)} %param.8), kind=kOutput, calls=%fused_computation.9 | convolution fusion | flops 1811939328 | bytes 3293184 | tf_op jit(solution)/shard_map/dot_general | solution.py:177
  57.3 0.1 pad.15.clone
  57.4 0.6 copy-done.9
  58.0 0.1 copy-done.7
  58.1 0.6 copy-done.8
  58.7 3.0 %shard_map.69 = f32[32,4,8,128]{3,2,1,0:T(8,128)} custom-call(f32[32,4,8,128]{3,2,1,0:T(8,128)} %get-tuple-element.24.scaled, f32[4,8,128]{2,1,0:T(8,128)} %theta.5, f32[4,8,128]{2,1,0:T(8,128)} %reaction.3, f32[32,8,128]{2,1,0:T(8,128)} %copy-done.7, f32[32,8,128]{2,1,0:T(8,128)} %copy-done.8, f32[32,4,128]{2,1,0:T(4,128)} %copy-done.9, ...), custom_call_target="tpu_custom_call" | custom-call | flops 4194304 | bytes 2097152 | tf_op jit(solution)/shard_map/pallas_call | solution.py:128
  61.7 5.4 %fusion.11 = f32[32,192]{1,0:T(8,128)S(1)} fusion(f32[192,4,8,128]{3,2,1,0:T(8,128)S(1)} %copy-done, f32[32,4,8,128]{3,2,1,0:T(8,128)} %shard_map.69), kind=kOutput, calls=%fused_computation.12 | convolution fusion | flops 301989888 | bytes 3694592 | tf_op jit(solution)/shard_map/dot_general | solution.py:177
  67.1 0.8 convolution_bitcast_fusion
  67.9 0.1 maximum_maximum_fusion
  68.0 10.8 %all_to_all.20 = f32[8,40,128]{2,1,0:T(8,128)S(1)} all-to-all(f32[8,40,128]{2,1,0:T(8,128)S(1)} %bitcast.66), channel_id=1, replica_groups=mesh['y'=8,'core'=2,'gy'=8,'gz'=4] {'core','gz'}, dimensions={0} | all-to-all | bytes 327680 | tf_op jit(solution)/shard_map/all_to_all | solution.py:154
  78.8 20.7 %all_to_all.21 = f32[8,40,128]{2,1,0:T(8,128)S(1)} all-to-all(f32[8,40,128]{2,1,0:T(8,128)S(1)} %broadcast_in_dim.9), channel_id=1, replica_groups=mesh['y'=8,'core'=2,'gy'=8,'gz'=4] {'gy'}, dimensions={0} | all-to-all | bytes 327680 | tf_op jit(solution)/shard_map/all_to_all | solution.py:148
  99.6 18.7 %all_to_all.22 = f32[8,40,128]{2,1,0:T(8,128)S(1)} all-to-all(f32[8,40,128]{2,1,0:T(8,128)S(1)} %broadcast_in_dim.10), channel_id=1, replica_groups=mesh['y'=8,'core'=2,'gy'=8,'gz'=4] {'y'}, dimensions={0} | all-to-all | bytes 327680 | tf_op jit(solution)/shard_map/all_to_all | solution.py:148
  118.4 11.0 %all_to_all.23 = f32[8,40,128]{2,1,0:T(8,128)S(1)} all-to-all(f32[8,40,128]{2,1,0:T(8,128)S(1)} %broadcast_in_dim.11), channel_id=1, replica_groups=mesh['y'=8,'core'=2,'gy'=8,'gz'=4] {'core','gz'}, dimensions={0} | all-to-all | bytes 327680 | tf_op jit(solution)/shard_map/all_to_all | solution.py:157
  129.5 0.7 slice.63
  130.1 0.1 copy.44
  130.2 0.6 pad_maximum_fusion.3
  130.8 0.9 copy.45
  131.8 0.9 convolution_subtract_fusion.2
  132.7 1.3 fusion.45
  134.1 0.8 convolution_subtract_fusion.1
  134.9 0.1 slice.61
  135.0 0.1 copy.56
  135.0 1.0 convolution_subtract_fusion.4
  136.0 0.9 convolution_subtract_fusion.3
  137.0 0.1 copy.48
  137.0 2.9 %cholesky.44 = f32[32,32]{1,0:T(8,128)S(1)} custom-call(f32[32,32]{1,0:T(8,128)S(1)} %fusion.24), custom_call_target="Cholesky" | custom-call | tf_op jit(solution)/shard_map/jit(cholesky)/cholesky | solution.py:211
  140.0 0.6 compare_reduce_fusion.1
  140.6 0.7 fusion.28
  141.3 2.4 %custom-call.6 = f32[1,32,32]{1,2,0:T(8,128)S(1)} custom-call(f32[1,32,32]{2,1,0:T(8,128)S(1)} %fusion.28), custom_call_target="InvertDiagBlocksLowerTriangular" | custom-call | tf_op jit(solution)/shard_map/jit(_solve_triangular)/triangular_solve | solution.py:212
  143.7 0.2 fusion.22
  144.0 0.1 fusion.50
  144.1 0.2 fusion.51
  144.3 0.1 copy.49
  144.4 2.9 %cholesky.55 = f32[32,32]{1,0:T(8,128)S(1)} custom-call(f32[32,32]{1,0:T(8,128)S(1)} %fusion.21), custom_call_target="Cholesky" | custom-call | tf_op jit(solution)/shard_map/jit(cholesky)/cholesky | solution.py:214
  147.3 0.7 compare_reduce_fusion
  148.0 2.1 %fusion.33 = f32[32,32]{1,0:T(8,128)} fusion(f32[32,32]{1,0:T(8,128)S(1)} %cholesky.55, f32[32,32]{1,0:T(8,128)S(1)} %cholesky.44, pred[]{:T(512)} %compare_reduce_fusion, pred[]{:T(512)} %compare_reduce_fusion.1), kind=kOutput, calls=%fused_computation.49 | convolution fusion | flops 399360 | bytes 12290 | tf_op jit(solution)/shard_map/dot_general | solution.py:177
  150.1 0.6 select_bitcast_fusion
  150.7 2.4 %custom-call.7 = f32[1,32,32]{1,2,0:T(8,128)S(1)} custom-call(f32[1,32,32]{2,1,0:T(8,128)S(1)} %select_bitcast_fusion), custom_call_target="InvertDiagBlocksLowerTriangular" | custom-call | tf_op jit(solution)/shard_map/jit(_solve_triangular)/triangular_solve | solution.py:215
  153.2 0.2 fusion.19
  153.4 0.9 fusion.46
  154.3 3.7 %fusion = f32[32,4096]{1,0:T(8,128)S(1)} fusion(f32[32,192]{1,0:T(8,128)S(1)} %fusion.46, f32[24,8,32,128]{3,2,1,0:T(8,128)S(1)} %bitcast.58), kind=kOutput, calls=%fused_computation.1 | convolution fusion | flops 301989888 | bytes 3694592 | tf_op jit(solution)/shard_map/dot_general | solution.py:177
  158.0 0.9 fusion.7
  158.9 0.9 copy.59
  (53 shorter events, 0.3 us)
Async XLA Ops:
  2.6 21.7 %collective-permute-start = (f32[33,8,128]{2,1,0:T(8,128)}, f32[33,8,128]{2,1,0:T(8,128)S(1)}, u32[]{:S(2)}, u32[]{:S(2)}) collective-permute-start(f32[33,8,128]{2,1,0:T(8,128)} %get-tuple-element.18), channel_id=1, source_target_pairs={{0,32},{32,64},{64,96},{96,128},{128,160},{160,192},{192,224},{224... | collective-permute-start | bytes 405512 | tf_op jit(solution)/shard_map/ppermute | solution.py:18
  7.2 17.7 %collective-permute-start.1 = (f32[33,8,128]{2,1,0:T(8,128)}, f32[33,8,128]{2,1,0:T(8,128)S(1)}, u32[]{:S(2)}, u32[]{:S(2)}) collective-permute-start(f32[33,8,128]{2,1,0:T(8,128)} %get-tuple-element.19), channel_id=1, source_target_pairs={{32,0},{64,32},{96,64},{128,96},{160,128},{192,160},{224,192},{256... | collective-permute-start | bytes 405512 | tf_op jit(solution)/shard_map/ppermute | solution.py:18
  12.6 11.6 %collective-permute-start.2 = (f32[33,4,128]{2,1,0:T(4,128)}, f32[33,4,128]{2,1,0:T(4,128)S(1)}, u32[]{:S(2)}, u32[]{:S(2)}) collective-permute-start(f32[33,4,128]{2,1,0:T(4,128)} %get-tuple-element.20), channel_id=1, source_target_pairs={{0,4},{4,8},{8,12},{12,16},{16,20},{20,24},{24,28},{1,5},{5,9},{9,... | collective-permute-start | bytes 202760 | tf_op jit(solution)/shard_map/ppermute | solution.py:18
  13.9 10.3 %collective-permute-start.3 = (f32[33,4,128]{2,1,0:T(4,128)}, f32[33,4,128]{2,1,0:T(4,128)S(1)}, u32[]{:S(2)}, u32[]{:S(2)}) collective-permute-start(f32[33,4,128]{2,1,0:T(4,128)} %get-tuple-element.21), channel_id=1, source_target_pairs={{4,0},{8,4},{12,8},{16,12},{20,16},{24,20},{28,24},{5,1},{9,5},{13... | collective-permute-start | bytes 202760 | tf_op jit(solution)/shard_map/ppermute | solution.py:18
  15.2 3.3 %collective-permute-start.4 = (f32[16,128]{1,0:T(8,128)}, f32[16,128]{1,0:T(8,128)S(1)}, u32[]{:S(2)}, u32[]{:S(2)}) collective-permute-start(f32[16,128]{1,0:T(8,128)} %get-tuple-element.22), channel_id=1, source_target_pairs={{0,1},{1,2},{2,3},{4,5},{5,6},{6,7},{8,9},{9,10},{10,11},{12,13},{... | collective-permute-start | bytes 24584 | tf_op jit(solution)/shard_map/ppermute | solution.py:18
  18.5 0.6 copy-start.11
  19.1 42.6 %copy-start = (f32[192,4,8,128]{3,2,1,0:T(8,128)S(1)}, f32[192,4,8,128]{3,2,1,0:T(8,128)}, u32[]{:S(2)}) copy-start(f32[192,4,8,128]{3,2,1,0:T(8,128)} %param.8) | copy-start | bytes 9437188
  19.1 5.1 %collective-permute-start.5 = (f32[16,128]{1,0:T(8,128)}, f32[16,128]{1,0:T(8,128)S(1)}, u32[]{:S(2)}, u32[]{:S(2)}) collective-permute-start(f32[16,128]{1,0:T(8,128)} %get-tuple-element.23), channel_id=1, source_target_pairs={{1,0},{2,1},{3,2},{5,4},{6,5},{7,6},{9,8},{10,9},{11,10},{13,12},{... | collective-permute-start | bytes 24584 | tf_op jit(solution)/shard_map/ppermute | solution.py:18
  24.2 0.6 copy-start.12
  24.2 0.6 copy-start.5
  24.2 0.6 copy-start.6
  24.8 0.7 copy-start.3
  25.5 0.7 copy-start.4
  29.3 17.7 %collective-permute-start.10 = (f32[8,128]{1,0:T(8,128)}, f32[8,128]{1,0:T(8,128)S(1)}, u32[]{:S(2)}, u32[]{:S(2)}) collective-permute-start(f32[8,128]{1,0:T(8,128)} %get-tuple-element.29), channel_id=1, source_target_pairs={{0,1},{1,2},{2,3},{4,5},{5,6},{6,7},{8,9},{9,10},{10,11},{12,13},{... | collective-permute-start | bytes 12296 | tf_op jit(solution)/shard_map/ppermute | solution.py:18
  32.9 24.5 %collective-permute-start.6 = (f32[32,8,128]{2,1,0:T(8,128)}, f32[32,8,128]{2,1,0:T(8,128)S(1)}, u32[]{:S(2)}, u32[]{:S(2)}) collective-permute-start(f32[32,8,128]{2,1,0:T(8,128)} %get-tuple-element.25), channel_id=1, source_target_pairs={{0,32},{32,64},{64,96},{96,128},{128,160},{160,192},{192,224},{224... | collective-permute-start | bytes 393224 | tf_op jit(solution)/shard_map/ppermute | solution.py:18
  39.2 18.2 %collective-permute-start.7 = (f32[32,8,128]{2,1,0:T(8,128)}, f32[32,8,128]{2,1,0:T(8,128)S(1)}, u32[]{:S(2)}, u32[]{:S(2)}) collective-permute-start(f32[32,8,128]{2,1,0:T(8,128)} %get-tuple-element.26), channel_id=1, source_target_pairs={{32,0},{64,32},{96,64},{128,96},{160,128},{192,160},{224,192},{256... | collective-permute-start | bytes 393224 | tf_op jit(solution)/shard_map/ppermute | solution.py:18
  41.1 16.2 %collective-permute-start.8 = (f32[32,4,128]{2,1,0:T(4,128)}, f32[32,4,128]{2,1,0:T(4,128)S(1)}, u32[]{:S(2)}, u32[]{:S(2)}) collective-permute-start(f32[32,4,128]{2,1,0:T(4,128)} %get-tuple-element.27), channel_id=1, source_target_pairs={{0,4},{4,8},{8,12},{12,16},{16,20},{20,24},{24,28},{1,5},{5,9},{9,... | collective-permute-start | bytes 196616 | tf_op jit(solution)/shard_map/ppermute | solution.py:18
  45.8 11.6 %collective-permute-start.9 = (f32[32,4,128]{2,1,0:T(4,128)}, f32[32,4,128]{2,1,0:T(4,128)S(1)}, u32[]{:S(2)}, u32[]{:S(2)}) collective-permute-start(f32[32,4,128]{2,1,0:T(4,128)} %get-tuple-element.28), channel_id=1, source_target_pairs={{4,0},{8,4},{12,8},{16,12},{20,16},{24,20},{28,24},{5,1},{9,5},{13... | collective-permute-start | bytes 196616 | tf_op jit(solution)/shard_map/ppermute | solution.py:18
  47.1 10.9 %copy-start.13 = (f32[8,128]{1,0:T(8,128)}, f32[8,128]{1,0:T(8,128)S(1)}, u32[]{:S(2)}) copy-start(f32[8,128]{1,0:T(8,128)S(1)} %collective-permute-done.10.refs_4_) | copy-start | bytes 12292
  47.1 10.3 %collective-permute-start.11 = (f32[8,128]{1,0:T(8,128)}, f32[8,128]{1,0:T(8,128)S(1)}, u32[]{:S(2)}, u32[]{:S(2)}) collective-permute-start(f32[8,128]{1,0:T(8,128)} %get-tuple-element.30), channel_id=1, source_target_pairs={{1,0},{2,1},{3,2},{5,4},{6,5},{7,6},{9,8},{10,9},{11,10},{13,12},{... | collective-permute-start | bytes 12296 | tf_op jit(solution)/shard_map/ppermute | solution.py:18
  57.4 0.7 copy-start.14
  57.4 0.6 copy-start.9
  57.4 0.6 copy-start.10
  57.4 0.7 copy-start.7
  58.0 0.6 copy-start.8
  61.7 5.4 %copy-start.1 = (f32[32,4,8,128]{3,2,1,0:T(8,128)S(1)}, f32[32,4,8,128]{3,2,1,0:T(8,128)}, u32[]{:S(2)}) copy-start(f32[32,4,8,128]{3,2,1,0:T(8,128)} %shard_map.69) | copy-start | bytes 1572868
  153.2 4.8 %copy-start.2 = (f32[32,4,8,128]{3,2,1,0:T(8,128)S(1)}, f32[32,4,8,128]{3,2,1,0:T(8,128)}, u32[]{:S(2)}) copy-start(f32[32,4,8,128]{3,2,1,0:T(8,128)} %shard_map.69) | copy-start | bytes 1572868
